TPU v7x, 32 devices: a whole 2x2x4 slice. The times are simulated.
32 devices in a mesh: dp: 8 (over z, y), tensor: 4 (over x, core).
Axes of the slice: x: 2, y: 2, z: 4, core: 2. Of those that a mesh axis runs over, the one named last changes fastest.
Arguments:
- inputs: bfloat16 [8192, 1536], P('dp', 'tensor'), may hold values from -6 to 6
- segment_ids: int32 [8192], P('dp'), may hold values from 0 to 26, never falling along the last dimension, each value on 1 to 1000 neighbouring positions
- cotangent: bfloat16 [8192, 1536], P('dp', 'tensor'), may hold values from -6 to 6
- first_gain: bfloat16 [1536], replicated, may hold values from 0.5 to 1.5
- gate_weight: bfloat16 [1536, 2048], P(None, 'tensor'), may hold values from -0.15625 to 0.15625
- gate_bias: bfloat16 [2048], P('tensor'), may hold values from -3 to 3
- branch_weight: bfloat16 [1536, 2048], P(None, 'tensor'), may hold values from -0.15625 to 0.15625
- branch_bias: bfloat16 [2048], P('tensor'), may hold values from -3 to 3
- conv_weight: bfloat16 [4, 2048], P(None, 'tensor'), may hold values from -3 to 3
- conv_bias: bfloat16 [2048], P('tensor'), may hold values from -3 to 3
- rate_weight: bfloat16 [16, 128, 128], P('tensor'), may hold values from -0.5 to 0.5
- rate_bias: bfloat16 [2048], P('tensor'), may hold values from -3 to 3
- input_weight: bfloat16 [16, 128, 128], P('tensor'), may hold values from -0.5 to 0.5
- input_bias: bfloat16 [2048], P('tensor'), may hold values from -3 to 3
- decay_param: float32 [2048], P('tensor'), may hold values from 3 to 7
- out_weight: bfloat16 [2048, 1536], P('tensor'), may hold values from -0.25 to 0.25
- second_gain: bfloat16 [1536], replicated, may hold values from 0.5 to 1.5
- ffn_gate: bfloat16 [1536, 4608], P(None, 'tensor'), may hold values from -0.15625 to 0.15625
- ffn_up: bfloat16 [1536, 4608], P(None, 'tensor'), may hold values from -0.15625 to 0.15625
- ffn_down: bfloat16 [4608, 1536], P('tensor'), may hold values from -0.1875 to 0.1875
Outputs:
- output: bfloat16 [8192, 1536], P('dp', 'tensor')
- input_grad: float32 [8192, 1536], P('dp', 'tensor')
- first_gain_grad: float32 [1536], replicated
- gate_weight_grad: float32 [1536, 2048], P(None, 'tensor')
- gate_bias_grad: float32 [2048], P('tensor')
- branch_weight_grad: float32 [1536, 2048], P(None, 'tensor')
- branch_bias_grad: float32 [2048], P('tensor')
- conv_weight_grad: float32 [4, 2048], P(None, 'tensor')
- conv_bias_grad: float32 [2048], P('tensor')
- rate_weight_grad: float32 [16, 128, 128], P('tensor')
- rate_bias_grad: float32 [2048], P('tensor')
- input_weight_grad: float32 [16, 128, 128], P('tensor')
- input_bias_grad: float32 [2048], P('tensor')
- decay_grad: float32 [2048], P('tensor')
- out_weight_grad: float32 [2048, 1536], P('tensor')
- second_gain_grad: float32 [1536], replicated
- ffn_gate_grad: float32 [1536, 4608], P(None, 'tensor')
- ffn_up_grad: float32 [1536, 4608], P(None, 'tensor')
- ffn_down_grad: float32 [4608, 1536], P('tensor')
Inputs may be any that keep to these rules, and one draw needn't show every extreme that they name: `segment_ids`: segment numbers never fall along the tokens; each document has 1 to 1000 consecutive tokens, one exactly 1000.
All inputs are finite; a program needn't handle non-finite values.
Results may differ from a plain program's by a relative error of at most 0.013.
Values may be sent and summed in bfloat16 or wider, within the bound.
A program may use at most 256 MiB of HBM per device.

v0:
```python
import jax
import jax.numpy as jnp
from jax import lax
from jax.sharding import PartitionSpec as P

SEQ = 1024
EPSILON = 1e-06
FLOOR = 0.05


def rms_scale(values, gain):
    return values * lax.rsqrt(jnp.mean(values * values, axis=-1, keepdims=True) + EPSILON) * gain


def seq_masks(segments, length):
    count = segments.shape[0]
    place = jnp.arange(count, dtype=jnp.int32) % length
    previous = jnp.concatenate([segments[:1], segments[:-1]])
    reset = (place == 0) | (segments != previous)
    return (place, reset)


def conv_apply(values, weights, shift_bias, segments, place):
    total = shift_bias + weights[0] * values
    for offset in range(1, weights.shape[0]):
        moved = jnp.concatenate(
            [jnp.zeros((offset, values.shape[1]), values.dtype), values[:-offset]]
        )
        earlier = jnp.concatenate([jnp.full((offset,), -1, jnp.int32), segments[:-offset]])
        usable = ((place >= offset) & (segments == earlier)).astype(values.dtype)
        total = total + weights[offset] * moved * usable[:, None]
    return total


def gates_to_step(rate_pre, input_pre, conv_out, decay, reset):
    rate = jax.nn.sigmoid(rate_pre)
    opened = jax.nn.sigmoid(input_pre)
    decayed = jnp.exp(-8.0 * rate * jax.nn.softplus(-decay))
    keep = jnp.where(reset[:, None], jnp.zeros_like(decayed), decayed)
    scale = jnp.where(
        reset[:, None],
        jnp.ones_like(decayed),
        jnp.sqrt(jnp.maximum(1.0 - decayed * decayed, FLOOR)),
    )
    return (keep, scale * opened * conv_out)


def combine(earlier, later):
    return (earlier[0] * later[0], later[0] * earlier[1] + later[1])


def block_mix(values, weight):
    rows = values.shape[0]
    split = values.reshape(rows, weight.shape[0], -1)
    return jnp.einsum("thi,hij->thj", split, weight, preferred_element_type=jnp.float32).reshape(
        rows, -1
    )


def block_back(grads, weight):
    rows = grads.shape[0]
    split = grads.reshape(rows, weight.shape[0], -1)
    return jnp.einsum("thj,hij->thi", split, weight, preferred_element_type=jnp.float32).reshape(
        rows, -1
    )


def block_grad(values, grads, heads):
    rows = values.shape[0]
    left = values.reshape(rows, heads, -1)
    right = grads.reshape(rows, heads, -1)
    return jnp.einsum("thi,thj->hij", left, right, preferred_element_type=jnp.float32)


def column_sum(values):
    return jnp.sum(values.astype(jnp.float32), axis=0)


def body(
    inputs,
    segment_ids,
    cotangent,
    first_gain,
    gate_weight,
    gate_bias,
    branch_weight,
    branch_bias,
    conv_weight,
    conv_bias,
    rate_weight,
    rate_bias,
    input_weight,
    input_bias,
    decay_param,
    out_weight,
    second_gain,
    ffn_gate,
    ffn_up,
    ffn_down,
):
    share = inputs.shape[1]
    heads = rate_weight.shape[0]
    offset = lax.axis_index("tensor") * share
    place, reset = seq_masks(segment_ids, SEQ)
    whole_in = lax.all_gather(inputs, "tensor", axis=1, tiled=True).astype(jnp.float32)
    normed_one, first_pull = jax.vjp(rms_scale, whole_in, first_gain.astype(jnp.float32))
    normed_low = normed_one.astype(jnp.bfloat16)
    gate_pre = jnp.dot(
        normed_low, gate_weight, preferred_element_type=jnp.float32
    ) + gate_bias.astype(jnp.float32)
    branch_pre = jnp.dot(
        normed_low, branch_weight, preferred_element_type=jnp.float32
    ) + branch_bias.astype(jnp.float32)

    def conv_local(values, weights, shift_bias):
        return conv_apply(values, weights, shift_bias, segment_ids, place)

    conv_out, conv_pull = jax.vjp(
        conv_local, branch_pre, conv_weight.astype(jnp.float32), conv_bias.astype(jnp.float32)
    )
    conv_low = conv_out.astype(jnp.bfloat16)
    rate_pre = block_mix(conv_low, rate_weight) + rate_bias.astype(jnp.float32)
    input_pre = block_mix(conv_low, input_weight) + input_bias.astype(jnp.float32)

    def step_local(rate_in, input_in, driven, decay):
        return gates_to_step(rate_in, input_in, driven, decay, reset)

    (keep, drive), step_pull = jax.vjp(step_local, rate_pre, input_pre, conv_out, decay_param)
    state = lax.associative_scan(combine, (keep, drive))[1]
    gate_act, gelu_pull = jax.vjp(jax.nn.gelu, gate_pre)
    mixed_low = (gate_act * state).astype(jnp.bfloat16)
    partial_value = jnp.dot(mixed_low, out_weight, preferred_element_type=jnp.float32)
    resid = whole_in + lax.psum(partial_value, "tensor")
    resid_mine = lax.dynamic_slice_in_dim(resid, offset, share, 1)
    normed_two, second_pull = jax.vjp(rms_scale, resid, second_gain.astype(jnp.float32))
    two_low = normed_two.astype(jnp.bfloat16)
    hidden_gate = jnp.dot(two_low, ffn_gate, preferred_element_type=jnp.float32)
    hidden_up = jnp.dot(two_low, ffn_up, preferred_element_type=jnp.float32)
    hidden_act, hidden_pull = jax.vjp(jax.nn.gelu, hidden_gate)
    hidden_low = (hidden_act * hidden_up).astype(jnp.bfloat16)
    ffn_part = jnp.dot(hidden_low, ffn_down, preferred_element_type=jnp.float32)
    output = (
        resid_mine
        + lax.psum_scatter(
            ffn_part.astype(jnp.bfloat16), "tensor", scatter_dimension=1, tiled=True
        ).astype(jnp.float32)
    ).astype(jnp.bfloat16)
    whole_cot = lax.all_gather(cotangent, "tensor", axis=1, tiled=True)
    d_hidden = jnp.einsum("td,fd->tf", whole_cot, ffn_down, preferred_element_type=jnp.float32)
    ffn_down_grad = jnp.einsum(
        "tf,td->fd", hidden_low, whole_cot, preferred_element_type=jnp.float32
    )
    d_hgate = hidden_pull(d_hidden * hidden_up)[0].astype(jnp.bfloat16)
    d_hup = (d_hidden * hidden_act).astype(jnp.bfloat16)
    ffn_gate_grad = jnp.einsum("td,tf->df", two_low, d_hgate, preferred_element_type=jnp.float32)
    ffn_up_grad = jnp.einsum("td,tf->df", two_low, d_hup, preferred_element_type=jnp.float32)
    d_two_part = jnp.einsum(
        "tf,df->td", d_hgate, ffn_gate, preferred_element_type=jnp.float32
    ) + jnp.einsum("tf,df->td", d_hup, ffn_up, preferred_element_type=jnp.float32)
    d_two = lax.psum(d_two_part, "tensor")
    d_resid_norm, second_gain_grad = second_pull(d_two)
    d_resid = whole_cot.astype(jnp.float32) + d_resid_norm
    d_resid_low = d_resid.astype(jnp.bfloat16)
    out_weight_grad = jnp.einsum(
        "tr,td->rd", mixed_low, d_resid_low, preferred_element_type=jnp.float32
    )
    d_mixed = jnp.einsum("td,rd->tr", d_resid_low, out_weight, preferred_element_type=jnp.float32)
    d_gate_low = gelu_pull(d_mixed * state)[0].astype(jnp.bfloat16)
    d_state = d_mixed * gate_act
    channels = keep.shape[1]
    keep_next = jnp.concatenate([keep[1:], jnp.zeros((1, channels), jnp.float32)])
    adjoint = lax.associative_scan(combine, (keep_next, d_state), reverse=True)[1]
    state_prev = jnp.concatenate([jnp.zeros((1, channels), jnp.float32), state[:-1]])
    d_rate, d_input, d_conv_direct, decay_grad = step_pull((adjoint * state_prev, adjoint))
    d_rate_low = d_rate.astype(jnp.bfloat16)
    d_input_low = d_input.astype(jnp.bfloat16)
    rate_weight_grad = block_grad(conv_low, d_rate_low, heads)
    input_weight_grad = block_grad(conv_low, d_input_low, heads)
    rate_bias_grad = column_sum(d_rate_low)
    input_bias_grad = column_sum(d_input_low)
    d_conv = (
        d_conv_direct + block_back(d_rate_low, rate_weight) + block_back(d_input_low, input_weight)
    )
    d_branch, conv_weight_grad, conv_bias_grad = conv_pull(d_conv)
    d_branch_low = d_branch.astype(jnp.bfloat16)
    gate_weight_grad = jnp.einsum(
        "td,tr->dr", normed_low, d_gate_low, preferred_element_type=jnp.float32
    )
    branch_weight_grad = jnp.einsum(
        "td,tr->dr", normed_low, d_branch_low, preferred_element_type=jnp.float32
    )
    gate_bias_grad = column_sum(d_gate_low)
    branch_bias_grad = column_sum(d_branch_low)
    d_first_part = jnp.einsum(
        "tr,dr->td", d_gate_low, gate_weight, preferred_element_type=jnp.float32
    ) + jnp.einsum("tr,dr->td", d_branch_low, branch_weight, preferred_element_type=jnp.float32)
    d_first = lax.psum(d_first_part.astype(jnp.bfloat16), "tensor").astype(jnp.float32)
    d_in_norm, first_gain_grad = first_pull(d_first)
    input_grad = lax.dynamic_slice_in_dim(d_resid + d_in_norm, offset, share, 1)
    pieces = (
        lax.psum_scatter(first_gain_grad, "dp", scatter_dimension=0, tiled=True),
        lax.psum_scatter(gate_weight_grad, "dp", scatter_dimension=0, tiled=True),
        lax.psum_scatter(gate_bias_grad, "dp", scatter_dimension=0, tiled=True),
        lax.psum_scatter(branch_weight_grad, "dp", scatter_dimension=0, tiled=True),
        lax.psum_scatter(branch_bias_grad, "dp", scatter_dimension=0, tiled=True),
        lax.psum_scatter(conv_weight_grad, "dp", scatter_dimension=1, tiled=True),
        lax.psum_scatter(conv_bias_grad, "dp", scatter_dimension=0, tiled=True),
        lax.psum_scatter(rate_weight_grad, "dp", scatter_dimension=1, tiled=True),
        lax.psum_scatter(rate_bias_grad, "dp", scatter_dimension=0, tiled=True),
        lax.psum_scatter(input_weight_grad, "dp", scatter_dimension=1, tiled=True),
        lax.psum_scatter(input_bias_grad, "dp", scatter_dimension=0, tiled=True),
        lax.psum_scatter(decay_grad, "dp", scatter_dimension=0, tiled=True),
        lax.psum_scatter(out_weight_grad, "dp", scatter_dimension=0, tiled=True),
        lax.psum_scatter(second_gain_grad, "dp", scatter_dimension=0, tiled=True),
        lax.psum_scatter(ffn_gate_grad, "dp", scatter_dimension=0, tiled=True),
        lax.psum_scatter(ffn_up_grad, "dp", scatter_dimension=0, tiled=True),
        lax.psum_scatter(ffn_down_grad, "dp", scatter_dimension=1, tiled=True),
    )
    done = (
        lax.all_gather(pieces[0].astype(jnp.bfloat16), "dp", axis=0, tiled=True).astype(
            jnp.float32
        ),
        lax.all_gather(pieces[1].astype(jnp.bfloat16), "dp", axis=0, tiled=True).astype(
            jnp.float32
        ),
        lax.all_gather(pieces[2].astype(jnp.bfloat16), "dp", axis=0, tiled=True).astype(
            jnp.float32
        ),
        lax.all_gather(pieces[3].astype(jnp.bfloat16), "dp", axis=0, tiled=True).astype(
            jnp.float32
        ),
        lax.all_gather(pieces[4].astype(jnp.bfloat16), "dp", axis=0, tiled=True).astype(
            jnp.float32
        ),
        lax.all_gather(pieces[5].astype(jnp.bfloat16), "dp", axis=1, tiled=True).astype(
            jnp.float32
        ),
        lax.all_gather(pieces[6].astype(jnp.bfloat16), "dp", axis=0, tiled=True).astype(
            jnp.float32
        ),
        lax.all_gather(pieces[7].astype(jnp.bfloat16), "dp", axis=1, tiled=True).astype(
            jnp.float32
        ),
        lax.all_gather(pieces[8].astype(jnp.bfloat16), "dp", axis=0, tiled=True).astype(
            jnp.float32
        ),
        lax.all_gather(pieces[9].astype(jnp.bfloat16), "dp", axis=1, tiled=True).astype(
            jnp.float32
        ),
        lax.all_gather(pieces[10].astype(jnp.bfloat16), "dp", axis=0, tiled=True).astype(
            jnp.float32
        ),
        lax.all_gather(pieces[11].astype(jnp.bfloat16), "dp", axis=0, tiled=True).astype(
            jnp.float32
        ),
        lax.all_gather(pieces[12].astype(jnp.bfloat16), "dp", axis=0, tiled=True).astype(
            jnp.float32
        ),
        lax.all_gather(pieces[13].astype(jnp.bfloat16), "dp", axis=0, tiled=True).astype(
            jnp.float32
        ),
        lax.all_gather(pieces[14].astype(jnp.bfloat16), "dp", axis=0, tiled=True).astype(
            jnp.float32
        ),
        lax.all_gather(pieces[15].astype(jnp.bfloat16), "dp", axis=0, tiled=True).astype(
            jnp.float32
        ),
        lax.all_gather(pieces[16].astype(jnp.bfloat16), "dp", axis=1, tiled=True).astype(
            jnp.float32
        ),
    )
    return (
        output,
        input_grad,
        done[0],
        done[1],
        done[2],
        done[3],
        done[4],
        done[5],
        done[6],
        done[7],
        done[8],
        done[9],
        done[10],
        done[11],
        done[12],
        done[13],
        done[14],
        done[15],
        done[16],
    )


def solution(mesh):
    in_specs = (
        P("dp", "tensor"),
        P("dp"),
        P("dp", "tensor"),
        P(),
        P(None, "tensor"),
        P("tensor"),
        P(None, "tensor"),
        P("tensor"),
        P(None, "tensor"),
        P("tensor"),
        P("tensor", None, None),
        P("tensor"),
        P("tensor", None, None),
        P("tensor"),
        P("tensor"),
        P("tensor", None),
        P(),
        P(None, "tensor"),
        P(None, "tensor"),
        P("tensor", None),
    )
    out_specs = (
        P("dp", "tensor"),
        P("dp", "tensor"),
        P(),
        P(None, "tensor"),
        P("tensor"),
        P(None, "tensor"),
        P("tensor"),
        P(None, "tensor"),
        P("tensor"),
        P("tensor", None, None),
        P("tensor"),
        P("tensor", None, None),
        P("tensor"),
        P("tensor"),
        P("tensor", None),
        P(),
        P(None, "tensor"),
        P(None, "tensor"),
        P("tensor", None),
    )
    return jax.shard_map(body, mesh=mesh, in_specs=in_specs, out_specs=out_specs, check_vma=False)
```

profile of v0, /device:TPU:0, one launch (start us, length us, event | category | flops | bytes accessed | tf_op | source)
XLA Modules:
  0.0 2209.8 jit_solution(8797544625298831027)
XLA Ops:
  21.3 19.5 all-gather.10.cloned.1.call-done
  207.6 6.3 slice.533
  214.0 6.3 slice.606
  284.1 8.6 pad.169
  296.5 8.6 pad.168
  305.1 8.0 multiply_convert_fusion.4
  319.4 118.9 %all-reduce.76.cloned.1.call-done = f32[1024,1536]{1,0:T(8,128)} async-done(((f32[1024,1536]{1,0:T(8,128)}), f32[1024,1536]{1,0:T(8,128)}) %all-reduce.76.cloned.1.call-update) | async-done | bytes 6291472 | tf_op jit(solution)/shard_map/psum | solution.py:133
  458.9 9.7 all-gather.12.cloned.1.call-done
  468.6 12.3 multiply_convert_fusion.2
  494.9 6.7 slice.611
  514.1 8.9 slice.612
  523.0 8.9 slice.619
  531.8 9.1 slice.610
  545.0 66.2 %all-reduce.78.cloned.1.call-done = f32[1024,1536]{1,0:T(8,128)} async-done(((f32[1024,1536]{1,0:T(8,128)}), f32[1024,1536]{1,0:T(8,128)}) %all-reduce.78.cloned.1.call-update) | async-done | bytes 6291472 | tf_op jit(solution)/shard_map/psum | solution.py:160
  640.8 8.9 slice.614
  649.7 8.9 slice.616
  840.5 8.5 pad.189
  849.0 9.1 slice.688
  861.9 8.5 pad.188
  874.5 16.6 rev.2
  891.1 8.4 multiply_reduce_fusion.5
  913.1 6.7 multiply_reduce_fusion.9
  930.1 6.6 fusion.24
  942.8 9.9 fusion.123
  952.8 10.0 fusion.124
  963.2 9.9 fusion.125
  987.1 7.3 add_convert_fusion
  994.5 7.3 convolution_convert_fusion
  1008.3 73.4 %reduce-scatter.23.cloned.1.call-done = f32[64,1536]{1,0:T(8,128)} async-done(((f32[512,1536]{1,0:T(8,128)}), f32[64,1536]{1,0:T(8,128)}) %reduce-scatter.23.cloned.1.call-update) | async-done | bytes 393232 | tf_op jit(solution)/shard_map/reduce_scatter | solution.py:213
  1083.5 75.9 %reduce-scatter.15.cloned.1.call-done = f32[192,512]{1,0:T(8,128)} async-done(((f32[1536,512]{1,0:T(8,128)}), f32[192,512]{1,0:T(8,128)}) %reduce-scatter.15.cloned.1.call-update) | async-done | bytes 393232 | tf_op jit(solution)/shard_map/reduce_scatter | solution.py:202
  1161.3 130.8 %reduce-scatter.25.cloned.1.call-done = f32[192,1152]{1,0:T(8,128)} async-done(((f32[1536,1152]{1,0:T(8,128)}), f32[192,1152]{1,0:T(8,128)}) %reduce-scatter.25.cloned.1.call-update) | async-done | bytes 884752 | tf_op jit(solution)/shard_map/reduce_scatter | solution.py:215
  1294.1 130.5 %reduce-scatter.27.cloned.1.call-done = f32[192,1152]{1,0:T(8,128)} async-done(((f32[1536,1152]{1,0:T(8,128)}), f32[192,1152]{1,0:T(8,128)}) %reduce-scatter.27.cloned.1.call-update) | async-done | bytes 884752 | tf_op jit(solution)/shard_map/reduce_scatter | solution.py:216
  1426.7 130.4 %reduce-scatter.29.cloned.1.call-done = f32[1152,192]{0,1:T(8,128)} async-done(((f32[1152,1536]{0,1:T(8,128)}), f32[1152,192]{0,1:T(8,128)}) %reduce-scatter.29.cloned.1.call-update) | async-done | bytes 884752 | tf_op jit(solution)/shard_map/reduce_scatter | solution.py:217
  1567.7 54.5 %reduce-scatter.33.cloned.1.call-done = f32[64,4]{1,0:T(8,128)} async-done(((f32[512,4]{1,0:T(8,128)}), f32[64,4]{1,0:T(8,128)}) %reduce-scatter.33.cloned.1.call-update) | async-done | bytes 1040
  1623.0 18.6 all-gather
  1642.3 45.2 %reduce-scatter.19.cloned.1.call-done = f32[4,16,128]{2,1,0:T(8,128)} async-done(((f32[4,128,128]{2,1,0:T(8,128)}), f32[4,16,128]{2,1,0:T(8,128)}) %reduce-scatter.19.cloned.1.call-update) | async-done | bytes 32784 | tf_op jit(solution)/shard_map/reduce_scatter | solution.py:208
  1688.3 30.6 %all_gather.66 = bf16[4,128,128]{2,1,0:T(8,128)(2,1)S(1)} all-gather(bf16[4,16,128]{2,1,0:T(8,128)(2,1)S(1)} %convert_element_type.250), channel_id=1, replica_groups=mesh['dp'=8,'tensor'=4] {'dp'}, dimensions={1}, use_global_device_ids=true | all-gather | bytes 147456 | tf_op jit(solution)/shard_map/all_gather | solution.py:241
  1719.6 33.4 %reduce-scatter.21.cloned.1.call-done = f32[4,16,128]{2,1,0:T(8,128)} async-done(((f32[4,128,128]{2,1,0:T(8,128)}), f32[4,16,128]{2,1,0:T(8,128)}) %reduce-scatter.21.cloned.1.call-update) | async-done | bytes 32784 | tf_op jit(solution)/shard_map/reduce_scatter | solution.py:210
  1753.7 30.8 %all_gather.68 = bf16[4,128,128]{2,1,0:T(8,128)(2,1)S(1)} all-gather(bf16[4,16,128]{2,1,0:T(8,128)(2,1)S(1)} %convert_element_type.255), channel_id=1, replica_groups=mesh['dp'=8,'tensor'=4] {'dp'}, dimensions={1}, use_global_device_ids=true | all-gather | bytes 147456 | tf_op jit(solution)/shard_map/all_gather | solution.py:247
  1785.2 38.1 %all-reduce.80.cloned.1.call-done = bf16[1024,1536]{1,0:T(8,128)(2,1)} async-done(((bf16[1024,1536]{1,0:T(8,128)(2,1)}), bf16[1024,1536]{1,0:T(8,128)(2,1)}) %all-reduce.80.cloned.1.call-update) | async-done | bytes 3145744 | tf_op jit(solution)/shard_map/psum | solution.py:197
  1823.3 6.8 fusion
  1830.2 38.4 %all-reduce.70 = (bf16[1536]{0:T(1024)(128)(2,1)}, bf16[512]{0:T(512)(128)(2,1)}, bf16[512]{0:T(512)(128)(2,1)}, bf16[512]{0:T(512)(128)(2,1)}, bf16[512]{0:T(51...) all-reduce(f32[1536]{0:T(1024)} %get-tuple-element.116, ...), channel_id=3, replica_groups=mesh['dp'=8,'tensor'=4] {'dp'}, use_global_device_ids=true, to_apply=%region_9.10.clone | all-reduce | flops 6144 | bytes 36864
  1887.8 34.5 %all-reduce.71 = (bf16[1536]{0:T(1024)(128)(2,1)}, bf16[512]{0:T(512)(128)(2,1)}, bf16[512]{0:T(512)(128)(2,1)}, bf16[512]{0:T(512)(128)(2,1)}, bf16[512]{0:T(51...) all-reduce(bf16[1536]{0:T(1024)(128)(2,1)S(1)} %dynamic-update-slic, ...), channel_id=1, replica_groups=mesh['dp'=8,'tensor'=4] {'dp'}, use_global_device_ids=true, to_apply=%add.54 | all-reduce | flops 6144 | bytes 24576
  1945.6 10.5 all-gather.18.cloned.1.call-done
  1959.6 41.1 %all-gather.14.cloned.1.call-done = bf16[1536,512]{1,0:T(8,128)(2,1)} async-done(((bf16[192,512]{1,0:T(8,128)(2,1)}), bf16[1536,512]{1,0:T(8,128)(2,1)}) %all-gather.14.cloned.1.call-update) | async-done | bytes 1572880 | tf_op jit(solution)/shard_map/all_gather | solution.py:223
  2004.2 61.7 %all-gather.20.cloned.1.call-done = bf16[1536,1152]{1,0:T(8,128)(2,1)} async-done(((bf16[192,1152]{1,0:T(8,128)(2,1)}), bf16[1536,1152]{1,0:T(8,128)(2,1)}) %all-gather.20.cloned.1.call-update) | async-done | bytes 3538960 | tf_op jit(solution)/shard_map/all_gather | solution.py:262
  2071.3 60.0 %all-gather.22.cloned.1.call-done = bf16[1536,1152]{1,0:T(8,128)(2,1)} async-done(((bf16[192,1152]{1,0:T(8,128)(2,1)}), bf16[1536,1152]{1,0:T(8,128)(2,1)}) %all-gather.22.cloned.1.call-update) | async-done | bytes 3538960 | tf_op jit(solution)/shard_map/all_gather | solution.py:265
  2136.7 60.1 %all-gather.24.cloned.1.call-done = bf16[1152,1536]{0,1:T(8,128)(2,1)} async-done(((bf16[1152,192]{0,1:T(8,128)(2,1)}), bf16[1152,1536]{0,1:T(8,128)(2,1)}) %all-gather.24.cloned.1.call-update) | async-done | bytes 3538960 | tf_op jit(solution)/shard_map/all_gather | solution.py:268
  (541 shorter events, 661.8 us)
Async XLA Ops:
  7.2 461.4 %copy-start = (bf16[1152,1536]{1,0:T(8,128)(2,1)S(1)}, bf16[1152,1536]{1,0:T(8,128)(2,1)}, u32[]{:S(2)}) copy-start(bf16[1152,1536]{1,0:T(8,128)(2,1)} %param.39) | copy-start | bytes 10616836
  7.2 33.6 %all-gather.10.cloned.1.call-start = ((), (), s32[]{:S(2)}) async-start(), calls=%async_computation.10 | async-start | bytes 3932160 | tf_op jit(solution)/shard_map/all_gather | solution.py:105
  7.9 430.4 %all-reduce.76.cloned.1.call-start = ((), (), s32[]{:S(2)}) async-start(), calls=%async_computation.11 | async-start | bytes 12582912 | tf_op jit(solution)/shard_map/psum | solution.py:133
  13.9 51.3 %copy-start.15 = (f32[512]{0:T(512)}, f32[512]{0:T(512)S(1)}, u32[]{:S(2)}) copy-start(f32[512]{0:T(512)S(1)} %convert_element_type.215) | copy-start | bytes 6148
  21.3 26.2 %copy-start.17 = (f32[1024]{0:T(1024)}, f32[1024]{0:T(1024)S(1)}, u32[]{:S(2)}) copy-start(f32[1024]{0:T(1024)S(1)} %get-tuple-element.209) | copy-start | bytes 12292
  21.3 26.2 %copy-start.19 = (f32[1024]{0:T(1024)}, f32[1024]{0:T(1024)S(1)}, u32[]{:S(2)}) copy-start(f32[1024]{0:T(1024)S(1)} %get-tuple-element.214) | copy-start | bytes 12292
  21.3 26.2 %copy-start.21 = (f32[1024]{0:T(1024)}, f32[1024]{0:T(1024)S(1)}, u32[]{:S(2)}) copy-start(f32[1024]{0:T(1024)S(1)} %get-tuple-element.215) | copy-start | bytes 12292
  207.6 14.0 copy-start.45
  207.6 14.0 copy-start.59
  234.8 18.4 copy-start.55
  253.2 11.0 copy-start.53
  296.5 8.6 copy-start.24
  296.5 8.6 copy-start.31
  296.5 8.6 copy-start.64
  305.1 9.0 copy-start.74
  318.6 150.0 %all-gather.12.cloned.1.call-start = ((), (), s32[]{:S(2)}) async-start(), calls=%async_computation.12 | async-start | bytes 3932160 | tf_op jit(solution)/shard_map/all_gather | solution.py:148
  319.3 291.9 %all-reduce.78.cloned.1.call-start = ((), (), s32[]{:S(2)}) async-start(), calls=%async_computation.13 | async-start | bytes 12582912 | tf_op jit(solution)/shard_map/psum | solution.py:160
  468.6 12.3 copy-start.71
  491.5 515.1 %reduce-scatter.17.cloned.1.call-start = ((), (), s32[]{:S(2)}) async-start(), calls=%async_computation.17 | async-start | bytes 3538944 | tf_op jit(solution)/shard_map/reduce_scatter | solution.py:204
  761.6 16.2 copy-start.46
  761.6 16.3 copy-start.60
  791.0 18.4 copy-start.56
  809.5 11.0 copy-start.54
  874.5 16.6 copy-start.16
  874.5 16.6 copy-start.34
  874.5 16.6 copy-start.36
  874.5 16.6 copy-start.48
  891.1 9.0 copy-start.4
  929.9 151.9 %reduce-scatter.23.cloned.1.call-start = ((), (), s32[]{:S(2)}) async-start(), calls=%async_computation.21 | async-start | bytes 3538944 | tf_op jit(solution)/shard_map/reduce_scatter | solution.py:213
  936.7 222.8 %reduce-scatter.15.cloned.1.call-start = ((), (), s32[]{:S(2)}) async-start(), calls=%async_computation.15 | async-start | bytes 3538944 | tf_op jit(solution)/shard_map/reduce_scatter | solution.py:202
  942.7 349.3 %reduce-scatter.25.cloned.1.call-start = ((), (), s32[]{:S(2)}) async-start(), calls=%async_computation.23 | async-start | bytes 7962624 | tf_op jit(solution)/shard_map/reduce_scatter | solution.py:215
  952.7 471.9 %reduce-scatter.27.cloned.1.call-start = ((), (), s32[]{:S(2)}) async-start(), calls=%async_computation.25 | async-start | bytes 7962624 | tf_op jit(solution)/shard_map/reduce_scatter | solution.py:216
  962.8 594.3 %reduce-scatter.29.cloned.1.call-start = ((), (), s32[]{:S(2)}) async-start(), calls=%async_computation.27 | async-start | bytes 7962624 | tf_op jit(solution)/shard_map/reduce_scatter | solution.py:217
  973.2 649.0 %reduce-scatter.33.cloned.1.call-start = ((), (), s32[]{:S(2)}) async-start(), calls=%async_computation.30 | async-start | bytes 294912
  975.4 712.1 %reduce-scatter.19.cloned.1.call-start = ((), (), s32[]{:S(2)}) async-start(), calls=%async_computation.19 | async-start | bytes 294912 | tf_op jit(solution)/shard_map/reduce_scatter | solution.py:208
  978.2 774.8 %reduce-scatter.21.cloned.1.call-start = ((), (), s32[]{:S(2)}) async-start(), calls=%async_computation.20 | async-start | bytes 294912 | tf_op jit(solution)/shard_map/reduce_scatter | solution.py:210
  987.1 836.3 %all-reduce.80.cloned.1.call-start = ((), (), s32[]{:S(2)}) async-start(), calls=%async_computation.14 | async-start | bytes 6291456 | tf_op jit(solution)/shard_map/psum | solution.py:197
  994.5 942.5 %reduce-scatter.31.cloned.1.call-start = ((), (), s32[]{:S(2)}) async-start(), calls=%async_computation.29 | async-start | bytes 3932160
  1006.5 935.6 %all-gather.16.cloned.1.call-start = ((), (), s32[]{:S(2)}) async-start(), calls=%async_computation.18 | async-start | bytes 1769472 | tf_op jit(solution)/shard_map/all_gather | solution.py:229
  1008.3 947.8 %all-gather.18.cloned.1.call-start = ((), (), s32[]{:S(2)}) async-start(), calls=%async_computation.22 | async-start | bytes 1769472 | tf_op jit(solution)/shard_map/all_gather | solution.py:256
  1083.5 917.2 %all-gather.14.cloned.1.call-start = ((), (), s32[]{:S(2)}) async-start(), calls=%async_computation.16 | async-start | bytes 1769472 | tf_op jit(solution)/shard_map/all_gather | solution.py:223
  1161.2 904.7 %all-gather.20.cloned.1.call-start = ((), (), s32[]{:S(2)}) async-start(), calls=%async_computation.24 | async-start | bytes 3981312 | tf_op jit(solution)/shard_map/all_gather | solution.py:262
  1294.1 265.0 %copy-start.63 = (u32[32]{0:T(128)S(1)}, u32[32]{0:T(128)}, u32[]{:S(2)}) copy-start(u32[32]{0:T(128)} %constant.193) | copy-start | bytes 388
  1294.1 837.2 %all-gather.22.cloned.1.call-start = ((), (), s32[]{:S(2)}) async-start(), calls=%async_computation.26 | async-start | bytes 3981312 | tf_op jit(solution)/shard_map/all_gather | solution.py:265
  1426.6 770.2 %all-gather.24.cloned.1.call-start = ((), (), s32[]{:S(2)}) async-start(), calls=%async_computation.28 | async-start | bytes 3981312 | tf_op jit(solution)/shard_map/all_gather | solution.py:268
  1785.2 45.0 %copy-start.29 = (f32[1536]{0:T(1024)S(1)}, f32[1536]{0:T(1024)}, u32[]{:S(2)}) copy-start(f32[1536]{0:T(1024)} %get-tuple-element.114) | copy-start | bytes 18436
  1785.2 147.2 %copy-start.28 = (f32[1024]{0:T(1024)S(1)}, f32[1024]{0:T(1024)}, u32[]{:S(2)}) copy-start(f32[1024]{0:T(1024)} %copy-done.27) | copy-start | bytes 12292
  1785.2 147.9 %copy-start.26 = (f32[1024]{0:T(1024)S(1)}, f32[1024]{0:T(1024)}, u32[]{:S(2)}) copy-start(f32[1024]{0:T(1024)} %copy-done.23) | copy-start | bytes 12292
  (53 other events, 187.3 us)
Sparse Core Ops, SparseCore 0:
  9.6 31.1 all-gather.9
  318.7 119.5 all-reduce.75
  439.9 28.6 all-gather.11
  491.6 119.5 all-reduce.77
  930.0 74.7 reduce-scatter.16
  1008.2 73.4 reduce-scatter.22
  1085.3 74.0 reduce-scatter.14
  1163.7 128.2 reduce-scatter.24
  1296.3 128.2 reduce-scatter.26
  1428.7 128.2 reduce-scatter.28
  1560.9 61.1 reduce-scatter.32
  1625.9 61.5 reduce-scatter.18
  1691.4 61.5 reduce-scatter.20
  1755.8 67.5 all-reduce.79
  1826.3 37.9 reduce-scatter.30
  1866.9 44.3 all-gather.15
  1913.4 42.6 all-gather.17
  1958.1 42.5 all-gather.13
  2002.9 62.9 all-gather.19
  2067.9 63.3 all-gather.21
  2133.5 63.3 all-gather.23
where the time goes:
time: 2230 us; the launch traced here: 2210 us
  waiting for transfers between devices  1160 us (52%)
  local copies, waits for them, and re-layouts  501 us (22%)
  other arithmetic  237 us (11%)
  blocking collectives  153 us (7%)
  matrix products  138 us (6%)
    slice x66, local copies, waits for them, and re-layouts, body(): lax.associative_scan(combine, (keep_next, d_state), reverse=True)[1]  185 us
    slice x60, local copies, waits for them, and re-layouts, body(): state = lax.associative_scan(combine, (keep, drive))[1]  131 us
    reduce_scatter x1, waiting for transfers between devices, body(): lax.psum_scatter(ffn_gate_grad, 'dp', scatter_dimension=0, tiled=True)  131 us
    reduce_scatter x1, waiting for transfers between devices, body(): lax.psum_scatter(ffn_up_grad, 'dp', scatter_dimension=0, tiled=True)  130 us
    reduce_scatter x1, waiting for transfers between devices, body(): lax.psum_scatter(ffn_down_grad, 'dp', scatter_dimension=1, tiled=True)  130 us
    psum x1, waiting for transfers between devices, body(): resid = whole_in + lax.psum(partial_value, 'tensor')  119 us
    reduce_scatter x1, waiting for transfers between devices, body(): lax.psum_scatter(gate_weight_grad, 'dp', scatter_dimension=0, tiled=True)  75.9 us
    reduce_scatter x1, waiting for transfers between devices, body(): lax.psum_scatter(out_weight_grad, 'dp', scatter_dimension=0, tiled=True)  73.4 us
  transfers between devices with their start and end apart: 21, of which 18 were waited for; matrix products, arithmetic and copies ran while one was open for 11% of the time, Pallas kernels for 0%

commit v1 on v0

--- a/solution.py
+++ b/solution.py
@@ -157,7 +157,17 @@
     d_two_part = jnp.einsum(
         "tf,df->td", d_hgate, ffn_gate, preferred_element_type=jnp.float32
     ) + jnp.einsum("tf,df->td", d_hup, ffn_up, preferred_element_type=jnp.float32)
-    d_two = lax.psum(d_two_part, "tensor")
+
+    def clear_slices_on_mesh(m):
+        dev_n = lax.axis_size("tensor")
+        block_next = m
+        for to_i in [
+            [(nth, nth ^ tick) for nth in range(dev_n)] for tick in (1, 2, 4, 8, 16) if tick < dev_n
+        ]:
+            block_next = block_next + lax.ppermute(block_next, "tensor", to_i)
+        return block_next
+
+    d_two = clear_slices_on_mesh(d_two_part)
     d_resid_norm, second_gain_grad = second_pull(d_two)
     d_resid = whole_cot.astype(jnp.float32) + d_resid_norm
     d_resid_low = d_resid.astype(jnp.bfloat16)

time: 2230 us -> 1890 us (0.85)
  waiting for transfers between devices: 1160 us -> 813 us
    reduce_scatter x1, waiting for transfers between devices: 131 us -> 0.02 us  [body(): lax.psum_scatter(ffn_gate_grad, 'dp', scatter_dimension=0, tiled=True)]
    reduce_scatter x1, waiting for transfers between devices: 130 us -> 0.02 us  [body(): lax.psum_scatter(ffn_up_grad, 'dp', scatter_dimension=0, tiled=True)]
    reduce_scatter x1, waiting for transfers between devices: 130 us -> 0.02 us  [body(): lax.psum_scatter(ffn_down_grad, 'dp', scatter_dimension=1, tiled=True)]
    ppermute x0 -> x2, waiting for transfers between devices: none -> 89.2 us  [clear_slices_on_mesh(): block_next = block_next + lax.ppermute(block_next, 'tensor', to_i)]
    psum x1 -> x0, waiting for transfers between devices: 66.2 us -> none  [body(): d_two = lax.psum(d_two_part, 'tensor')]
    all_gather x1, waiting for transfers between devices: 61.7 us -> 0.01 us  [body(): lax.all_gather(pieces[14].astype(jnp.bfloat16), 'dp', axis=0, tiled=True)]
    all_gather x1, waiting for transfers between devices: 60 us -> 11.9 us  [body(): lax.all_gather(pieces[15].astype(jnp.bfloat16), 'dp', axis=0, tiled=True)]
    all_gather x1, waiting for transfers between devices: 0.01 us -> 39 us  [body(): lax.all_gather(pieces[3].astype(jnp.bfloat16), 'dp', axis=0, tiled=True)]
  transfers between devices with their start and end apart: 21 -> 22, of which waited for: 18 -> 18; matrix products, arithmetic and copies ran while one was open for 11% -> 30% of each run, Pallas kernels for 0% -> 0%
where the time goes in v1:
time: 1890 us; the launch traced here: 1870 us
  waiting for transfers between devices  813 us (43%)
  local copies, waits for them, and re-layouts  501 us (27%)
  other arithmetic  246 us (13%)
  blocking collectives  155 us (8%)
  matrix products  132 us (7%)
    slice x66, local copies, waits for them, and re-layouts, body(): lax.associative_scan(combine, (keep_next, d_state), reverse=True)[1]  185 us
    slice x60, local copies, waits for them, and re-layouts, body(): state = lax.associative_scan(combine, (keep, drive))[1]  131 us
    psum x1, waiting for transfers between devices, body(): resid = whole_in + lax.psum(partial_value, 'tensor')  119 us
    unnamed x22, waiting for transfers between devices  92.2 us
    ppermute x2, waiting for transfers between devices, clear_slices_on_mesh(): block_next = block_next + lax.ppermute(block_next, 'tensor', to_i)  89.2 us
    reduce_scatter x1, waiting for transfers between devices, body(): lax.psum_scatter(gate_weight_grad, 'dp', scatter_dimension=0, tiled=True)  75.9 us
    reduce_scatter x1, waiting for transfers between devices, body(): lax.psum_scatter(out_weight_grad, 'dp', scatter_dimension=0, tiled=True)  75.3 us
    unnamed x2, blocking collectives  74.7 us
  transfers between devices with their start and end apart: 22, of which 18 were waited for; matrix products, arithmetic and copies ran while one was open for 30% of the time, Pallas kernels for 0%

profile of v1, /device:TPU:0, one launch (start us, length us, event | category | flops | bytes accessed | tf_op | source)
XLA Modules:
  0.0 1867.0 jit_solution(2670915282195766802)
XLA Ops:
  21.3 19.5 %all-gather.10.cloned.1.call-done = bf16[1024,1536]{1,0:T(8,128)(2,1)} async-done(((bf16[1024,384]{1,0:T(8,128)(2,1)}), bf16[1024,1536]{1,0:T(8,128)(2,1)}) %all-gather.10.cloned.1.call-update) | async-done | bytes 3145744 | tf_op jit(solution)/shard_map/all_gather | solution.py:105
  207.7 6.3 slice.533
  284.1 8.6 pad.169
  296.4 8.6 pad.168
  305.1 8.0 multiply_convert_fusion.4
  319.4 118.9 %all-reduce.75.cloned.1.call-done = f32[1024,1536]{1,0:T(8,128)} async-done(((f32[1024,1536]{1,0:T(8,128)}), f32[1024,1536]{1,0:T(8,128)}) %all-reduce.75.cloned.1.call-update) | async-done | bytes 6291472 | tf_op jit(solution)/shard_map/psum | solution.py:133
  458.9 9.7 all-gather.12.cloned.1.call-done
  468.6 12.6 multiply_convert_fusion.2
  489.0 9.9 fusion.124
  499.4 7.1 fusion.121
  511.2 9.9 collective-permute-done
  546.0 8.9 slice.612
  555.0 8.9 slice.619
  563.8 9.1 slice.610
  577.1 6.4 fusion.125
  583.8 79.2 %collective-permute-done.1 = f32[1024,1536]{1,0:T(8,128)} collective-permute-done((f32[1024,1536]{1,0:T(8,128)}, f32[1024,1536]{1,0:T(8,128)}, u32[]{:S(2)}, u32[]{:S(2)}) %collective-permute-start.1) | collective-permute-done | bytes 6291488 | tf_op jit(solution)/shard_map/ppermute | solution.py:167
  663.0 8.4 multiply_reduce_fusion
  671.5 7.7 fusion.1
  697.6 8.9 slice.614
  706.5 8.9 slice.616
  897.7 8.5 pad.189
  906.3 9.1 slice.688
  919.1 8.5 pad.188
  931.7 16.6 rev.2
  948.3 8.4 multiply_reduce_fusion.5
  970.3 6.7 multiply_reduce_fusion.9
  987.5 6.7 fusion.24
  1000.2 7.3 convolution_convert_fusion
  1026.1 7.1 add_convert_fusion
  1039.6 22.1 %reduce-scatter.17.cloned.1.call-done = f32[192,512]{1,0:T(8,128)} async-done(((f32[1536,512]{1,0:T(8,128)}), f32[192,512]{1,0:T(8,128)}) %reduce-scatter.17.cloned.1.call-update) | async-done | bytes 393232 | tf_op jit(solution)/shard_map/reduce_scatter | solution.py:214
  1063.4 75.3 %reduce-scatter.23.cloned.1.call-done = f32[64,1536]{1,0:T(8,128)} async-done(((f32[512,1536]{1,0:T(8,128)}), f32[64,1536]{1,0:T(8,128)}) %reduce-scatter.23.cloned.1.call-update) | async-done | bytes 393232 | tf_op jit(solution)/shard_map/reduce_scatter | solution.py:223
  1140.5 75.9 %reduce-scatter.15.cloned.1.call-done = f32[192,512]{1,0:T(8,128)} async-done(((f32[1536,512]{1,0:T(8,128)}), f32[192,512]{1,0:T(8,128)}) %reduce-scatter.15.cloned.1.call-update) | async-done | bytes 393232 | tf_op jit(solution)/shard_map/reduce_scatter | solution.py:212
  1227.0 29.4 %reduce-scatter.31.cloned.1.call-done = bf16[384,1024]{1,0:T(8,128)(2,1)} async-done(((bf16[1536,1024]{1,0:T(8,128)(2,1)}), bf16[384,1024]{1,0:T(8,128)(2,1)}) %reduce-scatter.31.cloned.1.call-update) | async-done | bytes 786448
  1261.4 61.1 %reduce-scatter.33.cloned.1.call-done = f32[64,4]{1,0:T(8,128)} async-done(((f32[512,4]{1,0:T(8,128)}), f32[64,4]{1,0:T(8,128)}) %reduce-scatter.33.cloned.1.call-update) | async-done | bytes 1040
  1323.3 18.6 all-gather
  1342.7 45.2 %reduce-scatter.19.cloned.1.call-done = f32[4,16,128]{2,1,0:T(8,128)} async-done(((f32[4,128,128]{2,1,0:T(8,128)}), f32[4,16,128]{2,1,0:T(8,128)}) %reduce-scatter.19.cloned.1.call-update) | async-done | bytes 32784 | tf_op jit(solution)/shard_map/reduce_scatter | solution.py:218
  1388.6 30.6 %all_gather.66 = bf16[4,128,128]{2,1,0:T(8,128)(2,1)S(1)} all-gather(bf16[4,16,128]{2,1,0:T(8,128)(2,1)S(1)} %convert_element_type.250), channel_id=1, replica_groups=mesh['dp'=8,'tensor'=4] {'dp'}, dimensions={1}, use_global_device_ids=true | all-gather | bytes 147456 | tf_op jit(solution)/shard_map/all_gather | solution.py:251
  1419.9 32.9 %reduce-scatter.21.cloned.1.call-done = f32[4,16,128]{2,1,0:T(8,128)} async-done(((f32[4,128,128]{2,1,0:T(8,128)}), f32[4,16,128]{2,1,0:T(8,128)}) %reduce-scatter.21.cloned.1.call-update) | async-done | bytes 32784 | tf_op jit(solution)/shard_map/reduce_scatter | solution.py:220
  1453.6 30.7 %all_gather.68 = bf16[4,128,128]{2,1,0:T(8,128)(2,1)S(1)} all-gather(bf16[4,16,128]{2,1,0:T(8,128)(2,1)S(1)} %convert_element_type.255), channel_id=1, replica_groups=mesh['dp'=8,'tensor'=4] {'dp'}, dimensions={1}, use_global_device_ids=true | all-gather | bytes 147456 | tf_op jit(solution)/shard_map/all_gather | solution.py:257
  1485.0 38.1 %all-reduce.77.cloned.1.call-done = bf16[1024,1536]{1,0:T(8,128)(2,1)} async-done(((bf16[1024,1536]{1,0:T(8,128)(2,1)}), bf16[1024,1536]{1,0:T(8,128)(2,1)}) %all-reduce.77.cloned.1.call-update) | async-done | bytes 3145744 | tf_op jit(solution)/shard_map/psum | solution.py:207
  1523.1 6.8 fusion
  1530.0 40.1 %all-reduce.70 = (bf16[1536]{0:T(1024)(128)(2,1)}, bf16[512]{0:T(512)(128)(2,1)}, bf16[512]{0:T(512)(128)(2,1)}, bf16[512]{0:T(512)(128)(2,1)}, bf16[512]{0:T(51...) all-reduce(f32[1536]{0:T(1024)} %get-tuple-element.116, ...), channel_id=3, replica_groups=mesh['dp'=8,'tensor'=4] {'dp'}, use_global_device_ids=true, to_apply=%region_8.9.clone | all-reduce | flops 6144 | bytes 36864
  1589.5 34.6 %all-reduce.71 = (bf16[1536]{0:T(1024)(128)(2,1)}, bf16[512]{0:T(512)(128)(2,1)}, bf16[512]{0:T(512)(128)(2,1)}, bf16[512]{0:T(512)(128)(2,1)}, bf16[512]{0:T(51...) all-reduce(bf16[1536]{0:T(1024)(128)(2,1)S(1)} %dynamic-update-slic, ...), channel_id=1, replica_groups=mesh['dp'=8,'tensor'=4] {'dp'}, use_global_device_ids=true, to_apply=%add.54 | all-reduce | flops 6144 | bytes 24576
  1644.2 11.9 all-gather.22.cloned.1.call-done
  1661.5 60.0 %all-gather.24.cloned.1.call-done = bf16[1152,1536]{0,1:T(8,128)(2,1)} async-done(((bf16[1152,192]{0,1:T(8,128)(2,1)}), bf16[1152,1536]{0,1:T(8,128)(2,1)}) %all-gather.24.cloned.1.call-update) | async-done | bytes 3538960 | tf_op jit(solution)/shard_map/all_gather | solution.py:278
  1727.5 39.0 %all-gather.16.cloned.1.call-done = bf16[1536,512]{1,0:T(8,128)(2,1)} async-done(((bf16[192,512]{1,0:T(8,128)(2,1)}), bf16[1536,512]{1,0:T(8,128)(2,1)}) %all-gather.16.cloned.1.call-update) | async-done | bytes 1572880 | tf_op jit(solution)/shard_map/all_gather | solution.py:239
  1770.0 41.2 %all-gather.18.cloned.1.call-done = bf16[512,1536]{1,0:T(8,128)(2,1)} async-done(((bf16[64,1536]{1,0:T(8,128)(2,1)}), bf16[512,1536]{1,0:T(8,128)(2,1)}) %all-gather.18.cloned.1.call-update) | async-done | bytes 1572880 | tf_op jit(solution)/shard_map/all_gather | solution.py:266
  1814.7 41.7 %all-gather.14.cloned.1.call-done = bf16[1536,512]{1,0:T(8,128)(2,1)} async-done(((bf16[192,512]{1,0:T(8,128)(2,1)}), bf16[1536,512]{1,0:T(8,128)(2,1)}) %all-gather.14.cloned.1.call-update) | async-done | bytes 1572880 | tf_op jit(solution)/shard_map/all_gather | solution.py:233
  (553 shorter events, 669.0 us)
Async XLA Ops:
  7.2 461.4 %copy-start = (bf16[1152,1536]{1,0:T(8,128)(2,1)S(1)}, bf16[1152,1536]{1,0:T(8,128)(2,1)}, u32[]{:S(2)}) copy-start(bf16[1152,1536]{1,0:T(8,128)(2,1)} %param.39) | copy-start | bytes 10616836
  7.2 33.6 %all-gather.10.cloned.1.call-start = ((), (), s32[]{:S(2)}) async-start(), calls=%async_computation.10 | async-start | bytes 3932160 | tf_op jit(solution)/shard_map/all_gather | solution.py:105
  7.9 430.4 %all-reduce.75.cloned.1.call-start = ((), (), s32[]{:S(2)}) async-start(), calls=%async_computation.11 | async-start | bytes 12582912 | tf_op jit(solution)/shard_map/psum | solution.py:133
  13.9 51.2 %copy-start.18 = (f32[512]{0:T(512)}, f32[512]{0:T(512)S(1)}, u32[]{:S(2)}) copy-start(f32[512]{0:T(512)S(1)} %convert_element_type.215) | copy-start | bytes 6148
  21.3 26.2 %copy-start.20 = (f32[1024]{0:T(1024)}, f32[1024]{0:T(1024)S(1)}, u32[]{:S(2)}) copy-start(f32[1024]{0:T(1024)S(1)} %get-tuple-element.209) | copy-start | bytes 12292
  21.3 26.2 %copy-start.22 = (f32[1024]{0:T(1024)}, f32[1024]{0:T(1024)S(1)}, u32[]{:S(2)}) copy-start(f32[1024]{0:T(1024)S(1)} %get-tuple-element.214) | copy-start | bytes 12292
  21.3 26.2 %copy-start.24 = (f32[1024]{0:T(1024)}, f32[1024]{0:T(1024)S(1)}, u32[]{:S(2)}) copy-start(f32[1024]{0:T(1024)S(1)} %get-tuple-element.215) | copy-start | bytes 12292
  207.7 14.0 copy-start.51
  207.7 14.0 copy-start.65
  234.7 18.4 copy-start.62
  253.2 11.0 copy-start.61
  305.1 9.0 copy-start.78
  318.6 150.0 %all-gather.12.cloned.1.call-start = ((), (), s32[]{:S(2)}) async-start(), calls=%async_computation.12 | async-start | bytes 3932160 | tf_op jit(solution)/shard_map/all_gather | solution.py:148
  319.3 714.0 %reduce-scatter.25.cloned.1.call-start = ((), (), s32[]{:S(2)}) async-start(), calls=%async_computation.22 | async-start | bytes 7962624 | tf_op jit(solution)/shard_map/reduce_scatter | solution.py:225
  468.6 14.0 copy-start.14
  489.0 546.4 %reduce-scatter.27.cloned.1.call-start = ((), (), s32[]{:S(2)}) async-start(), calls=%async_computation.24 | async-start | bytes 7962624 | tf_op jit(solution)/shard_map/reduce_scatter | solution.py:226
  498.9 538.6 %reduce-scatter.29.cloned.1.call-start = ((), (), s32[]{:S(2)}) async-start(), calls=%async_computation.26 | async-start | bytes 7962624 | tf_op jit(solution)/shard_map/reduce_scatter | solution.py:227
  510.8 14.6 copy-start.8
  510.9 10.2 collective-permute-start
  525.1 138.0 %collective-permute-start.1 = (f32[1024,1536]{1,0:T(8,128)}, f32[1024,1536]{1,0:T(8,128)}, u32[]{:S(2)}, u32[]{:S(2)}) collective-permute-start(f32[1024,1536]{1,0:T(8,128)} %add.517), channel_id=1, source_target_pairs={{0,2},{1,3},{2,0},{3,1},{4,6},{5,7},{6,4},{7,5},{8,10},{9,11},{10,... | collective-permute-start | bytes 18874376 | tf_op jit(solution)/shard_map/ppermute | solution.py:167
  583.6 478.1 %reduce-scatter.17.cloned.1.call-start = ((), (), s32[]{:S(2)}) async-start(), calls=%async_computation.16 | async-start | bytes 3538944 | tf_op jit(solution)/shard_map/reduce_scatter | solution.py:214
  815.4 16.3 copy-start.40
  815.4 16.3 copy-start.52
  815.4 19.6 %copy-start.17 = (f32[4,512]{1,0:T(4,128)S(1)}, f32[4,512]{1,0:T(4,128)}, u32[]{:S(2)}) copy-start(f32[4,512]{1,0:T(4,128)} %get-tuple-element.203) | copy-start | bytes 24580
  848.2 18.5 copy-start.59
  866.8 11.0 copy-start.58
  931.7 16.6 copy-start.19
  931.7 16.6 copy-start.37
  931.7 16.6 copy-start.39
  931.7 16.6 copy-start.54
  948.3 9.1 copy-start.4
  987.1 151.7 %reduce-scatter.23.cloned.1.call-start = ((), (), s32[]{:S(2)}) async-start(), calls=%async_computation.20 | async-start | bytes 3538944 | tf_op jit(solution)/shard_map/reduce_scatter | solution.py:223
  994.2 222.2 %reduce-scatter.15.cloned.1.call-start = ((), (), s32[]{:S(2)}) async-start(), calls=%async_computation.14 | async-start | bytes 3538944 | tf_op jit(solution)/shard_map/reduce_scatter | solution.py:212
  1000.1 256.3 %reduce-scatter.31.cloned.1.call-start = ((), (), s32[]{:S(2)}) async-start(), calls=%async_computation.28 | async-start | bytes 3932160
  1012.2 310.3 %reduce-scatter.33.cloned.1.call-start = ((), (), s32[]{:S(2)}) async-start(), calls=%async_computation.29 | async-start | bytes 294912
  1014.4 373.5 %reduce-scatter.19.cloned.1.call-start = ((), (), s32[]{:S(2)}) async-start(), calls=%async_computation.18 | async-start | bytes 294912 | tf_op jit(solution)/shard_map/reduce_scatter | solution.py:218
  1017.2 435.6 %reduce-scatter.21.cloned.1.call-start = ((), (), s32[]{:S(2)}) async-start(), calls=%async_computation.19 | async-start | bytes 294912 | tf_op jit(solution)/shard_map/reduce_scatter | solution.py:220
  1026.1 497.0 %all-reduce.77.cloned.1.call-start = ((), (), s32[]{:S(2)}) async-start(), calls=%async_computation.13 | async-start | bytes 6291456 | tf_op jit(solution)/shard_map/psum | solution.py:207
  1033.3 605.5 %all-gather.20.cloned.1.call-start = ((), (), s32[]{:S(2)}) async-start(), calls=%async_computation.23 | async-start | bytes 3981312 | tf_op jit(solution)/shard_map/all_gather | solution.py:272
  1035.4 620.8 %all-gather.22.cloned.1.call-start = ((), (), s32[]{:S(2)}) async-start(), calls=%async_computation.25 | async-start | bytes 3981312 | tf_op jit(solution)/shard_map/all_gather | solution.py:275
  1037.5 180.7 %copy-start.68 = (u32[32]{0:T(128)S(1)}, u32[32]{0:T(128)}, u32[]{:S(2)}) copy-start(u32[32]{0:T(128)} %constant.193) | copy-start | bytes 388
  1037.5 684.0 %all-gather.24.cloned.1.call-start = ((), (), s32[]{:S(2)}) async-start(), calls=%async_computation.27 | async-start | bytes 3981312 | tf_op jit(solution)/shard_map/all_gather | solution.py:278
  1039.6 726.9 %all-gather.16.cloned.1.call-start = ((), (), s32[]{:S(2)}) async-start(), calls=%async_computation.17 | async-start | bytes 1769472 | tf_op jit(solution)/shard_map/all_gather | solution.py:239
  1063.4 747.8 %all-gather.18.cloned.1.call-start = ((), (), s32[]{:S(2)}) async-start(), calls=%async_computation.21 | async-start | bytes 1769472 | tf_op jit(solution)/shard_map/all_gather | solution.py:266
  1140.5 716.0 %all-gather.14.cloned.1.call-start = ((), (), s32[]{:S(2)}) async-start(), calls=%async_computation.15 | async-start | bytes 1769472 | tf_op jit(solution)/shard_map/all_gather | solution.py:233
  1485.0 44.9 %copy-start.32 = (f32[1536]{0:T(1024)S(1)}, f32[1536]{0:T(1024)}, u32[]{:S(2)}) copy-start(f32[1536]{0:T(1024)} %get-tuple-element.114) | copy-start | bytes 18436
  1485.0 149.2 %copy-start.31 = (f32[1024]{0:T(1024)S(1)}, f32[1024]{0:T(1024)}, u32[]{:S(2)}) copy-start(f32[1024]{0:T(1024)} %copy-done.30) | copy-start | bytes 12292
  1485.0 149.8 %copy-start.29 = (f32[1024]{0:T(1024)S(1)}, f32[1024]{0:T(1024)}, u32[]{:S(2)}) copy-start(f32[1024]{0:T(1024)} %copy-done.26) | copy-start | bytes 12292
  (59 other events, 235.4 us)
Sparse Core Ops, SparseCore 0:
  9.6 31.1 all-gather.9
  318.7 119.5 all-reduce.74
  439.9 28.6 all-gather.11
  489.1 129.1 reduce-scatter.24
  622.4 128.2 reduce-scatter.26
  754.8 128.2 reduce-scatter.28
  987.2 74.4 reduce-scatter.16
  1065.3 73.4 reduce-scatter.22
  1142.9 73.4 reduce-scatter.14
  1219.4 37.0 reduce-scatter.30
  1260.3 62.1 reduce-scatter.32
  1326.3 61.5 reduce-scatter.18
  1391.2 61.5 reduce-scatter.20
  1455.6 67.4 all-reduce.76
  1525.2 65.2 all-gather.19
  1592.5 63.5 all-gather.21
  1658.1 63.3 all-gather.23
  1723.5 42.8 all-gather.15
  1768.7 42.5 all-gather.17
  1813.8 42.5 all-gather.13
